TPU v7x, 32 devices: a whole 2x2x4 slice. The times are simulated.
32 devices in a mesh: groups: 2 (over x), slab: 16 (over z, y, core).
Axes of the slice: x: 2, y: 2, z: 4, core: 2. Of those that a mesh axis runs over, the one named last changes fastest.
Arguments:
- activations: bfloat16 [2048, 65536], P(('groups', 'slab')), parts along dimension 0, may hold values from 0 to 4
- weights: bfloat16 [6, 2, 512, 128, 128], P(None, None, 'slab'), may hold values from -0.5 to 0.5
- biases: float32 [6, 65536], P(None, 'slab'), may hold values from -1 to 0.5
- columns: int32 [6, 512], P(None, 'slab'), may hold values from 0 to 31
Outputs:
- features: bfloat16 [2048, 65536], P(('groups', 'slab')), parts along dimension 0
There are 2 independent parts, one for each index of `groups`. A program takes and returns all parts, laid end to end along the dimension named above; an argument that names none is the same for every part. Nothing has to cross between parts.
Inputs may be any that keep to these rules, and one draw needn't show every extreme that they name: columns name a block within a group of 32 consecutive blocks.
All inputs are finite; a program needn't handle non-finite values.
Results may differ from a plain program's by a relative error of at most 0.0072.
Values may be sent and summed in bfloat16 or wider, within the bound.
No kernel may reach another device: no remote copies, remote signals or barrier semaphores. Data moves between devices by JAX's collectives and lax.ppermute only.
A program may use at most 128 MiB of HBM per device.

v0:
```python
import jax
import jax.numpy as jnp
from jax import lax
from jax.sharding import PartitionSpec as P

ceiling = 4.0


def from_partner(block, axis, bit):
    count = lax.axis_size(axis)
    route = []
    for low in range(count):
        high = low | 1 << bit
        if high != low and high < count:
            route += [(low, high), (high, low)]
    return lax.ppermute(block, axis, route)


def section_bit(section, remote, log_count):
    return (remote - 1 - section) * (log_count - 1) // (remote - 1)


def local(activations, weights, biases, columns):
    slab_count = lax.axis_size("slab")
    log_count = slab_count.bit_length() - 1
    layer_count = weights.shape[0]
    per_device = weights.shape[2]
    block_width = weights.shape[3]
    local_rows = activations.shape[0]
    remote = (layer_count + 1) // 2
    grouped = activations.reshape(local_rows, slab_count, per_device * block_width)
    stride = 1 << section_bit(0, remote, log_count)
    flipped = grouped.reshape(
        local_rows, slab_count // (2 * stride), 2, stride, per_device * block_width
    )
    flipped = flipped[:, :, ::-1].reshape(local_rows, slab_count, per_device * block_width)
    paired = jnp.stack([grouped, flipped], axis=2)
    arrived = lax.all_to_all(paired, "slab", split_axis=1, concat_axis=0, tiled=True)
    current = arrived[:, 0, 0].reshape(-1, per_device, block_width)
    first_cross = arrived[:, 0, 1].reshape(-1, per_device, block_width)
    for layer_index in range(layer_count):
        if layer_index % 2 == 0:
            if layer_index == 0 and first_cross is not None:
                source = first_cross
            else:
                source = from_partner(
                    current, "slab", section_bit(layer_index // 2, remote, log_count)
                )
        else:
            source = current
        crossing = jnp.take(source, columns[layer_index], axis=1)
        summed = jnp.einsum(
            "rkb,kbc->rkc", current, weights[layer_index, 0], preferred_element_type=jnp.float32
        )
        summed = summed + jnp.einsum(
            "rkb,kbc->rkc", crossing, weights[layer_index, 1], preferred_element_type=jnp.float32
        )
        summed = summed + biases[layer_index].reshape(per_device, block_width)
        current = jnp.clip(summed, 0.0, ceiling).astype(jnp.bfloat16)
    flattened = current.reshape(current.shape[0], per_device * block_width)
    return lax.all_to_all(flattened, "slab", split_axis=0, concat_axis=1, tiled=True)


def solution(mesh):
    placed = (
        P(("groups", "slab"), None),
        P(None, None, "slab", None, None),
        P(None, "slab"),
        P(None, "slab"),
    )
    return jax.shard_map(
        local, mesh=mesh, in_specs=placed, out_specs=P(("groups", "slab"), None), check_vma=False
    )
```

profile of v0, /device:TPU:1, one launch (start us, length us, event | category | flops | bytes accessed | tf_op | source)
XLA Modules:
  0.0 1066.5 jit_solution(5412748452448401006)
XLA Ops:
  0.0 12.1 %copy.28 = bf16[8,8,16,4096]{3,2,1,0:T(8,128)(2,1)} copy(bf16[8,8,16,4096]{3,1,2,0:T(8,128)(2,1)} %bitcast.134) | data formatting | bytes 16777216
  19.9 8.0 pad_maximum_fusion
  27.9 21.4 %copy.18 = bf16[64,16,2,4096]{3,0,2,1:T(8,128)(2,1)} copy(bf16[64,16,2,4096]{3,1,0,2:T(8,128)(2,1)S(1)} %pad_maximum_fusion) | data formatting | bytes 33554432 | tf_op jit(solution)/shard_map/stack | solution.py:37
  49.2 8.1 all-to-all-start
  58.6 295.9 %all-to-all-done = bf16[64,16,2,4096]{3,0,2,1:T(8,128)(2,1)} async-done(((bf16[64,16,2,4096]{3,0,2,1:T(8,128)(2,1)}), bf16[64,16,2,4096]{3,0,2,1:T(8,128)(2,1)}, u32[]{:S(2)}, u32[]{:S(2)}) %all-to-all-start) | async-done | bytes 16777248 | tf_op jit(solution)/shard_map/all_to_all | solution.py:38
  354.5 8.3 copy.19
  369.2 12.0 %copy.22 = bf16[1024,1,1,4096]{0,3,2,1:T(8,128)(2,1)} copy(bf16[1024,1,1,4096]{3,0,2,1:T(8,128)(2,1)} %get-tuple-element.18) | data formatting | bytes 16777216 | tf_op jit(solution)/shard_map/slice | solution.py:40
  381.1 11.4 %copy.23 = bf16[1024,32,128]{2,0,1:T(8,128)(2,1)} copy(bf16[1024,32,128]{0,2,1:T(8,128)(2,1)} %bitcast.132) | data formatting | bytes 16777216 | tf_op jit(solution)/shard_map/reshape;squeeze | solution.py:40
  392.5 11.9 %copy.20 = bf16[1024,1,1,4096]{0,3,2,1:T(8,128)(2,1)} copy(bf16[1024,1,1,4096]{3,0,2,1:T(8,128)(2,1)} %get-tuple-element.19) | data formatting | bytes 16777216 | tf_op jit(solution)/shard_map/slice | solution.py:39
  404.4 8.4 gather_fusion
  412.8 11.8 %fusion.58 = f32[32,1024,128]{2,1,0:T(8,128)} fusion(bf16[1024,32,128]{0,2,1:T(8,128)(2,1)} %bitcast.131, bf16[6,2,32,128,128]{4,3,2,1,0:T(8,128)(2,1)} %param.7), kind=kOutput, calls=%fused_computation.60 | convolution fusion | flops 1073741824 | bytes 26214400 | tf_op jit(solution)/shard_map/rkb,kbc->rkc/dot_general | solution.py:52
  424.6 13.5 %fusion.18 = bf16[1024,32,128]{2,0,1:T(8,128)(2,1)} fusion(f32[32,128]{1,0:T(8,128)S(1)} %bitcast.140, f32[32,1024,128]{2,1,0:T(8,128)} %fusion.58, bf16[32,1024,128]{2,1,0:T(8,128)(2,1)} %gather_fusion, pred[32]{0:T(512)(128)(4,1)S(1)} %get-tuple-element.32, bf16[6,2,32,128,128]{4,3,2,1,0:T(8,128)(2,1)} %param.7), kind=kOutput, calls=%fused_computation.32 | convolution fusion | flops 1094713344 | bytes 34619424 | tf_op jit(solution)/shard_map/rkb,kbc->rkc/dot_general | solution.py:55
  438.2 11.7 %fusion.55 = f32[32,1024,128]{2,1,0:T(8,128)} fusion(bf16[1024,32,128]{2,0,1:T(8,128)(2,1)} %fusion.18, bf16[6,2,32,128,128]{4,3,2,1,0:T(8,128)(2,1)} %param.7), kind=kOutput, calls=%fused_computation.57 | convolution fusion | flops 1073741824 | bytes 26214400 | tf_op jit(solution)/shard_map/rkb,kbc->rkc/dot_general | solution.py:52
  449.8 8.4 gather_fusion.1
  458.2 13.7 %fusion.21 = bf16[1024,32,128]{2,0,1:T(8,128)(2,1)} fusion(f32[32,128]{1,0:T(8,128)S(1)} %bitcast.139, f32[32,1024,128]{2,1,0:T(8,128)} %fusion.55, bf16[32,1024,128]{2,1,0:T(8,128)(2,1)} %gather_fusion.1, pred[32]{0:T(512)(128)(4,1)S(1)} %get-tuple-element.30, bf16[6,2,32,128,128]{4,3,2,1,0:T(8,128)(2,1)} %param.7), kind=kOutput, calls=%fused_computation.33 | convolution fusion | flops 1094713344 | bytes 34619424 | tf_op jit(solution)/shard_map/rkb,kbc->rkc/dot_general | solution.py:55
  471.9 22.8 %collective-permute-start = (bf16[1024,32,128]{2,0,1:T(8,128)(2,1)}, bf16[1024,32,128]{2,0,1:T(8,128)(2,1)}, u32[]{:S(2)}, u32[]{:S(2)}) collective-permute-start(bf16[1024,32,128]{2,0,1:T(8,128)(2,1)} %fusion.21), channel_id=1, source_target_pairs={{0,2},{2,0},{1,3},{3,1},{4,6},{6,4},{5,7},{7,5},{8,10},{10,8},{9,1... | collective-permute-start | bytes 25165832 | tf_op jit(solution)/shard_map/ppermute | solution.py:16
  494.7 11.7 %fusion.52 = f32[32,1024,128]{2,1,0:T(8,128)} fusion(bf16[1024,32,128]{2,0,1:T(8,128)(2,1)} %fusion.21, bf16[6,2,32,128,128]{4,3,2,1,0:T(8,128)(2,1)} %param.7), kind=kOutput, calls=%fused_computation.54 | convolution fusion | flops 1073741824 | bytes 26214400 | tf_op jit(solution)/shard_map/rkb,kbc->rkc/dot_general | solution.py:52
  506.4 169.1 %collective-permute-done = bf16[1024,32,128]{2,0,1:T(8,128)(2,1)} collective-permute-done((bf16[1024,32,128]{2,0,1:T(8,128)(2,1)}, bf16[1024,32,128]{2,0,1:T(8,128)(2,1)}, u32[]{:S(2)}, u32[]{:S(2)}) %collective-permute-start) | collective-permute-done | bytes 8388640 | tf_op jit(solution)/shard_map/ppermute | solution.py:16
  675.5 8.6 gather_fusion.2
  684.1 13.5 %fusion.24 = bf16[1024,32,128]{2,0,1:T(8,128)(2,1)} fusion(f32[32,128]{1,0:T(8,128)S(1)} %bitcast.138, f32[32,1024,128]{2,1,0:T(8,128)} %fusion.52, bf16[32,1024,128]{2,1,0:T(8,128)(2,1)} %gather_fusion.2, pred[32]{0:T(512)(128)(4,1)S(1)} %get-tuple-element.28, bf16[6,2,32,128,128]{4,3,2,1,0:T(8,128)(2,1)} %param.7), kind=kOutput, calls=%fused_computation.34 | convolution fusion | flops 1094713344 | bytes 34619424 | tf_op jit(solution)/shard_map/rkb,kbc->rkc/dot_general | solution.py:55
  697.6 11.7 %fusion.49 = f32[32,1024,128]{2,1,0:T(8,128)} fusion(bf16[1024,32,128]{2,0,1:T(8,128)(2,1)} %fusion.24, bf16[6,2,32,128,128]{4,3,2,1,0:T(8,128)(2,1)} %param.7), kind=kOutput, calls=%fused_computation.51 | convolution fusion | flops 1073741824 | bytes 26214400 | tf_op jit(solution)/shard_map/rkb,kbc->rkc/dot_general | solution.py:52
  709.3 8.5 gather_fusion.3
  717.8 13.5 %fusion.27 = bf16[1024,32,128]{2,0,1:T(8,128)(2,1)} fusion(f32[32,128]{1,0:T(8,128)S(1)} %bitcast.137, f32[32,1024,128]{2,1,0:T(8,128)} %fusion.49, bf16[32,1024,128]{2,1,0:T(8,128)(2,1)} %gather_fusion.3, pred[32]{0:T(512)(128)(4,1)S(1)} %get-tuple-element.26, bf16[6,2,32,128,128]{4,3,2,1,0:T(8,128)(2,1)} %param.7), kind=kOutput, calls=%fused_computation.35 | convolution fusion | flops 1094713344 | bytes 34619424 | tf_op jit(solution)/shard_map/rkb,kbc->rkc/dot_general | solution.py:55
  731.7 11.7 %fusion.46 = f32[32,1024,128]{2,1,0:T(8,128)} fusion(bf16[1024,32,128]{2,0,1:T(8,128)(2,1)} %fusion.27, bf16[6,2,32,128,128]{4,3,2,1,0:T(8,128)(2,1)} %param.7), kind=kOutput, calls=%fused_computation.48 | convolution fusion | flops 1073741824 | bytes 26214400 | tf_op jit(solution)/shard_map/rkb,kbc->rkc/dot_general | solution.py:52
  744.8 8.8 gather_fusion.4
  753.6 13.5 %fusion.30 = bf16[1024,32,128]{2,0,1:T(8,128)(2,1)} fusion(f32[32,128]{1,0:T(8,128)S(1)} %bitcast.136, f32[32,1024,128]{2,1,0:T(8,128)} %fusion.46, bf16[32,1024,128]{2,1,0:T(8,128)(2,1)} %gather_fusion.4, pred[32]{0:T(512)(128)(4,1)S(1)} %get-tuple-element.34, bf16[6,2,32,128,128]{4,3,2,1,0:T(8,128)(2,1)} %param.7), kind=kOutput, calls=%fused_computation.36 | convolution fusion | flops 1094713344 | bytes 34619424 | tf_op jit(solution)/shard_map/rkb,kbc->rkc/dot_general | solution.py:55
  767.1 11.7 %fusion.43 = f32[32,1024,128]{2,1,0:T(8,128)} fusion(bf16[1024,32,128]{2,0,1:T(8,128)(2,1)} %fusion.30, bf16[6,2,32,128,128]{4,3,2,1,0:T(8,128)(2,1)} %param.7), kind=kOutput, calls=%fused_computation.45 | convolution fusion | flops 1073741824 | bytes 26214400 | tf_op jit(solution)/shard_map/rkb,kbc->rkc/dot_general | solution.py:52
  778.8 8.6 gather_fusion.5
  787.4 13.7 %fusion.33 = bf16[1024,32,128]{2,0,1:T(8,128)(2,1)} fusion(f32[32,128]{1,0:T(8,128)S(1)} %bitcast.135, f32[32,1024,128]{2,1,0:T(8,128)} %fusion.43, bf16[32,1024,128]{2,1,0:T(8,128)(2,1)} %gather_fusion.5, pred[32]{0:T(512)(128)(4,1)S(1)} %copy-done.3, bf16[6,2,32,128,128]{4,3,2,1,0:T(8,128)(2,1)} %param.7), kind=kOutput, calls=%fused_computation.37 | convolution fusion | flops 1094713344 | bytes 34619424 | tf_op jit(solution)/shard_map/rkb,kbc->rkc/dot_general | solution.py:55
  801.1 12.2 %copy.24 = bf16[1024,32,128]{2,1,0:T(8,128)(2,1)} copy(bf16[1024,32,128]{2,0,1:T(8,128)(2,1)} %fusion.33) | data formatting | bytes 16777216 | tf_op jit(solution)/shard_map/convert_element_type | solution.py:59
  813.3 13.3 %all_to_all.31 = bf16[16,64,4096]{2,1,0:T(8,128)(2,1)} reshape(bf16[1024,32,128]{2,1,0:T(8,128)(2,1)} %copy.24) | data formatting | bytes 16777216 | tf_op jit(solution)/shard_map/all_to_all | solution.py:61
  826.6 231.7 %all_to_all.37 = bf16[16,64,4096]{2,1,0:T(8,128)(2,1)} all-to-all(bf16[16,64,4096]{2,1,0:T(8,128)(2,1)} %all_to_all.31), channel_id=1, replica_groups=mesh['groups'=2,'slab'=16] {'slab'}, dimensions={0} | all-to-all | bytes 16777216 | tf_op jit(solution)/shard_map/all_to_all | solution.py:61
  (18 shorter events, 25.1 us)
Async XLA Ops:
  49.2 8.2 copy-start.2
  49.2 8.7 copy-start
  49.2 305.2 %all-to-all-start = ((bf16[64,16,2,4096]{3,0,2,1:T(8,128)(2,1)}), bf16[64,16,2,4096]{3,0,2,1:T(8,128)(2,1)}, u32[]{:S(2)}, u32[]{:S(2)}) async-start(bf16[64,16,2,4096]{3,0,2,1:T(8,128)(2,1)} %copy.18), calls=%async_computation | async-start | bytes 33554432 | tf_op jit(solution)/shard_map/all_to_all | solution.py:38
  471.9 203.6 %collective-permute-start = (bf16[1024,32,128]{2,0,1:T(8,128)(2,1)}, bf16[1024,32,128]{2,0,1:T(8,128)(2,1)}, u32[]{:S(2)}, u32[]{:S(2)}) collective-permute-start(bf16[1024,32,128]{2,0,1:T(8,128)(2,1)} %fusion.21), channel_id=1, source_target_pairs={{0,2},{2,0},{1,3},{3,1},{4,6},{6,4},{5,7},{7,5},{8,10},{10,8},{9,1... | collective-permute-start | bytes 25165832 | tf_op jit(solution)/shard_map/ppermute | solution.py:16
  731.3 13.5 %collective-permute-start.1 = (bf16[1024,32,128]{2,0,1:T(8,128)(2,1)}, bf16[1024,32,128]{2,0,1:T(8,128)(2,1)}, u32[]{:S(2)}, u32[]{:S(2)}) collective-permute-start(bf16[1024,32,128]{2,0,1:T(8,128)(2,1)} %fusion.27), channel_id=1, source_target_pairs={{0,1},{1,0},{2,3},{3,2},{4,5},{5,4},{6,7},{7,6},{8,9},{9,8},{10,11... | collective-permute-start | bytes 25165832 | tf_op jit(solution)/shard_map/ppermute | solution.py:16
  778.8 8.6 copy-start.1
  778.8 8.6 copy-start.3
where the time goes:
time: 1070 us
  waiting for transfers between devices  466 us (44%)
  blocking collectives  232 us (22%)
  local copies, waits for them, and re-layouts  177 us (17%)
  matrix products  152 us (14%)
  starting transfers between devices  31.4 us (3%)
    all_to_all x1, waiting for transfers between devices, local(): lax.all_to_all(paired, 'slab', split_axis=1, concat_axis=0, tiled=True)  296 us
    all_to_all x1, blocking collectives, local(): lax.all_to_all(flattened, 'slab', split_axis=0, concat_axis=1, tiled=True)  232 us
    ppermute x2, waiting for transfers between devices, from_partner(): return lax.ppermute(block, axis, route)  171 us
    dot_general x6, matrix products, local(): jnp.einsum('rkb,kbc->rkc', crossing, weights[layer_index, 1], preferred_e...  81.4 us
    dot_general x6, matrix products, local(): jnp.einsum('rkb,kbc->rkc', current, weights[layer_index, 0], preferred_el...  70.2 us
    gather x6, local copies, waits for them, and re-layouts, local(): crossing = jnp.take(source, columns[layer_index], axis=1)  51.3 us
    another operation x2, local copies, waits for them, and re-layouts, local(): paired = jnp.stack([grouped, flipped], axis=2)  29.1 us
    ppermute x2, starting transfers between devices, from_partner(): return lax.ppermute(block, axis, route)  23.2 us
  transfers between devices with their start and end apart: 3, of which 3 were waited for; matrix products, arithmetic and copies ran while one was open for 2% of the time, Pallas kernels for 0%

commit v1 on v0

--- a/solution.py
+++ b/solution.py
@@ -4,6 +4,29 @@
 from jax.sharding import PartitionSpec as P
 
 ceiling = 4.0
+
+
+def in_blocks(x, dim, size):
+    before, after = (x.shape[:dim], x.shape[dim + 1 :])
+    return jnp.moveaxis(x.reshape(*before, size, -1, *after), dim, 0)
+
+
+def joined_along(pieces, dim):
+    lengths = list(pieces.shape[1:])
+    lengths[dim] *= pieces.shape[0]
+    return jnp.moveaxis(pieces, 0, dim).reshape(lengths)
+
+
+def rotated_exchange(value, axis, split_dim, concat_dim):
+    size, index = (lax.axis_size(axis), lax.axis_index(axis))
+    blocks = in_blocks(value, split_dim, size)
+    out = blocks
+    for lap in range(1, size):
+        target, source = ((index + lap) % size, (index - lap) % size)
+        sent = lax.dynamic_index_in_dim(blocks, target, 0)
+        theirs = lax.ppermute(sent, axis, [(i, (i + lap) % size) for i in range(size)])
+        out = lax.dynamic_update_slice_in_dim(out, theirs, source, axis=0)
+    return joined_along(out, concat_dim)
 
 
 def from_partner(block, axis, bit):
@@ -35,7 +58,7 @@
     )
     flipped = flipped[:, :, ::-1].reshape(local_rows, slab_count, per_device * block_width)
     paired = jnp.stack([grouped, flipped], axis=2)
-    arrived = lax.all_to_all(paired, "slab", split_axis=1, concat_axis=0, tiled=True)
+    arrived = rotated_exchange(paired, "slab", 1, 0)
     current = arrived[:, 0, 0].reshape(-1, per_device, block_width)
     first_cross = arrived[:, 0, 1].reshape(-1, per_device, block_width)
     for layer_index in range(layer_count):

time: 1070 us -> 1700 us (1.59); the launches traced: 1070 us -> 1680 us
  local copies, waits for them, and re-layouts: 177 us -> 816 us
  waiting for transfers between devices: 466 us -> 172 us
  starting transfers between devices: 31.4 us -> 276 us
  other arithmetic: 8.53 us -> 72.1 us
  blocking collectives: 232 us -> 187 us
    dynamic_update_slice x0 -> x16, local copies, waits for them, and re-layouts: none -> 578 us  [rotated_exchange(): out = lax.dynamic_update_slice_in_dim(out, theirs, source, axis=0)]
    all_to_all x1 -> x0, waiting for transfers between devices: 296 us -> none  [local(): lax.all_to_all(paired, 'slab', split_axis=1, concat_axis=0, tiled=True)]
    ppermute x0 -> x15, starting transfers between devices: none -> 275 us  [rotated_exchange(): lax.ppermute(sent, axis, [(i, (i + lap) % size) for i in range(size)])]
    another operation x1 -> x3, other arithmetic: 8 us -> 64.7 us  [local(): paired = jnp.stack([grouped, flipped], axis=2)]
    ppermute x0 -> x15, local copies, waits for them, and re-layouts: none -> 52.7 us  [rotated_exchange(): lax.ppermute(sent, axis, [(i, (i + lap) % size) for i in range(size)])]
    all_to_all x1, blocking collectives: 232 us -> 187 us  [local(): lax.all_to_all(flattened, 'slab', split_axis=0, concat_axis=1, tiled=True)]
    unnamed x9 -> x46, local copies, waits for them, and re-layouts: 12.2 us -> 49.1 us
    ppermute x2, starting transfers between devices: 23.2 us -> 1.23 us  [from_partner(): return lax.ppermute(block, axis, route)]
  transfers between devices with their start and end apart: 3 -> 17, of which waited for: 3 -> 2; matrix products, arithmetic and copies ran while one was open for 2% -> 41% of each run, Pallas kernels for 0% -> 0%
where the time goes in v1:
time: 1700 us; the launch traced here: 1680 us
  local copies, waits for them, and re-layouts  816 us (48%)
  starting transfers between devices  276 us (16%)
  blocking collectives  187 us (11%)
  waiting for transfers between devices  172 us (10%)
  matrix products  152 us (9%)
  other arithmetic  72.1 us (4%)
    dynamic_update_slice x16, local copies, waits for them, and re-layouts, rotated_exchange(): out = lax.dynamic_update_slice_in_dim(out, theirs, source, axis=0)  578 us
    ppermute x15, starting transfers between devices, rotated_exchange(): lax.ppermute(sent, axis, [(i, (i + lap) % size) for i in range(size)])  275 us
    all_to_all x1, blocking collectives, local(): lax.all_to_all(flattened, 'slab', split_axis=0, concat_axis=1, tiled=True)  187 us
    ppermute x2, waiting for transfers between devices, from_partner(): return lax.ppermute(block, axis, route)  172 us
    dot_general x6, matrix products, local(): jnp.einsum('rkb,kbc->rkc', crossing, weights[layer_index, 1], preferred_e...  81.7 us
    dot_general x6, matrix products, local(): jnp.einsum('rkb,kbc->rkc', current, weights[layer_index, 0], preferred_el...  70.4 us
    another operation x3, other arithmetic, local(): paired = jnp.stack([grouped, flipped], axis=2)  64.7 us
    ppermute x15, local copies, waits for them, and re-layouts, rotated_exchange(): lax.ppermute(sent, axis, [(i, (i + lap) % size) for i in range(size)])  52.7 us
  transfers between devices with their start and end apart: 17, of which 2 were waited for; matrix products, arithmetic and copies ran while one was open for 41% of the time, Pallas kernels for 0%

profile of v1, /device:TPU:1, one launch (start us, length us, event | category | flops | bytes accessed | tf_op | source)
XLA Modules:
  0.0 1675.4 jit_solution(3092649973864988160)
XLA Ops:
  19.9 25.5 %fusion.57 = (bf16[64,1,2,4096]{3,1,0,2:T(2,128)(2,1)S(1)}, bf16[64,1,2,4096]{3,1,0,2:T(2,128)(2,1)S(1)}, bf16[64,1,2,4096]{3,1,0,2:T(2,128)(2,1)S(1)}, bf16[64,...) fusion(s32[]{:T(128)S(6)} %select_n.278, ...), kind=kLoop, calls=%fused_computation.89 | loop fusion | flops 12582912 | bytes 23068696 | tf_op jit(solution)/shard_map/stack | solution.py:60
  62.9 26.9 %fusion.56 = (bf16[64,1,2,4096]{3,1,0,2:T(2,128)(2,1)}, bf16[64,1,2,4096]{3,1,0,2:T(2,128)(2,1)}, bf16[64,1,2,4096]{3,1,0,2:T(2,128)(2,1)}, bf16[64,1,2,4096]{3,...) fusion(s32[]{:T(128)S(6)} %select_n.274, bf16[64,16,1,4096]{3,1,0,2:T(8,128)(2,1)} %bitcast.175, ...), kind=kLoop, calls=%fused_computation.88 | loop fusion | flops 12582912 | bytes 23068696 | tf_op jit(solution)/shard_map/stack | solution.py:60
  109.0 16.6 collective-permute-start.8
  125.6 157.2 %collective-permute-start.9 = (bf16[1,64,1,2,4096]{4,1,3,2,0:T(8,128)(2,1)}, bf16[1,64,1,2,4096]{4,1,3,2,0:T(8,128)(2,1)}, u32[]{:S(2)}, u32[]{:S(2)}) collective-permute-start(bf16[1,64,1,2,4096]{4,1,3,2,0:T(8,128)(2,1)} %bitcast.187), channel_id=1, source_target_pairs={{0,10},{1,11},{2,12},{3,13},{4,14},{5,15},{6,0},{7,1},{8,2},{9,3},... | collective-permute-start | bytes 3145736 | tf_op jit(solution)/shard_map/ppermute | solution.py:27
  312.6 16.3 collective-permute-start.10
  329.0 22.0 %collective-permute-start.11 = (bf16[1,64,1,2,4096]{4,1,3,2,0:T(8,128)(2,1)}, bf16[1,64,1,2,4096]{4,1,3,2,0:T(8,128)(2,1)}, u32[]{:S(2)}, u32[]{:S(2)}) collective-permute-start(bf16[1,64,1,2,4096]{4,1,3,2,0:T(8,128)(2,1)} %bitcast.161), channel_id=1, source_target_pairs={{0,12},{1,13},{2,14},{3,15},{4,0},{5,1},{6,2},{7,3},{8,4},{9,5},{1... | collective-permute-start | bytes 3145736 | tf_op jit(solution)/shard_map/ppermute | solution.py:27
  350.9 34.0 %collective-permute-start.12 = (bf16[1,64,1,2,4096]{4,1,3,2,0:T(8,128)(2,1)}, bf16[1,64,1,2,4096]{4,1,3,2,0:T(8,128)(2,1)}, u32[]{:S(2)}, u32[]{:S(2)}) collective-permute-start(bf16[1,64,1,2,4096]{4,1,3,2,0:T(8,128)(2,1)} %bitcast.160), channel_id=1, source_target_pairs={{0,13},{1,14},{2,15},{3,0},{4,1},{5,2},{6,3},{7,4},{8,5},{9,6},{10... | collective-permute-start | bytes 3145736 | tf_op jit(solution)/shard_map/ppermute | solution.py:27
  384.9 18.3 %collective-permute-start.13 = (bf16[1,64,1,2,4096]{4,1,3,2,0:T(8,128)(2,1)}, bf16[1,64,1,2,4096]{4,1,3,2,0:T(8,128)(2,1)}, u32[]{:S(2)}, u32[]{:S(2)}) collective-permute-start(bf16[1,64,1,2,4096]{4,1,3,2,0:T(8,128)(2,1)} %bitcast.159), channel_id=1, source_target_pairs={{0,14},{1,15},{2,0},{3,1},{4,2},{5,3},{6,4},{7,5},{8,6},{9,7},{10,... | collective-permute-start | bytes 3145736 | tf_op jit(solution)/shard_map/ppermute | solution.py:27
  406.9 37.7 %dynamic_update_slice.45 = bf16[16,64,1,2,4096]{4,0,1,3,2:T(8,128)(2,1)} dynamic-update-slice(bf16[16,64,1,2,4096]{4,0,1,3,2:T(8,128)(2,1)} %fusion, bf16[1,64,1,2,4096]{4,0,1,3,2:T(2,128)(2,1)S(1)} %copy.40, s32[]{:T(128)S(6)} %select_n.224, s32[]{:T(128)} %constant.205.clone.1, s32[]{:T(128)} %constant.205.clone.1, s32[]{:T(128)} %constant.205.clone.1, s32[]{:T(128)} %constant.205.clone.1) | dynamic-update-slice | bytes 2097156 | tf_op jit(solution)/shard_map/dynamic_update_slice | solution.py:28
  448.2 37.5 %dynamic_update_slice.46 = bf16[16,64,1,2,4096]{4,0,1,3,2:T(8,128)(2,1)} dynamic-update-slice(bf16[16,64,1,2,4096]{4,0,1,3,2:T(8,128)(2,1)} %dynamic_update_slice.45, bf16[1,64,1,2,4096]{4,0,1,3,2:T(2,128)(2,1)S(1)} %copy.41, s32[]{:T(128)S(6)} %select_n.228, s32[]{:T(128)} %constant.205.clone.1, s32[]{:T(128)} %constant.205.clone.1, s32[]{:T(128)} %constant.205.clone.1, s32[]{:T(128)} %constant.205.clone.1) | dynamic-update-slice | bytes 2097156 | tf_op jit(solution)/shard_map/dynamic_update_slice | solution.py:28
  489.4 37.5 %dynamic_update_slice.47 = bf16[16,64,1,2,4096]{4,0,1,3,2:T(8,128)(2,1)} dynamic-update-slice(bf16[16,64,1,2,4096]{4,0,1,3,2:T(8,128)(2,1)} %dynamic_update_slice.46, bf16[1,64,1,2,4096]{4,0,1,3,2:T(2,128)(2,1)S(1)} %copy.42, s32[]{:T(128)S(6)} %select_n.232, s32[]{:T(128)} %constant.205.clone.1, s32[]{:T(128)} %constant.205.clone.1, s32[]{:T(128)} %constant.205.clone.1, s32[]{:T(128)} %constant.205.clone.1) | dynamic-update-slice | bytes 2097156 | tf_op jit(solution)/shard_map/dynamic_update_slice | solution.py:28
  530.5 37.5 %dynamic_update_slice.48 = bf16[16,64,1,2,4096]{4,0,1,3,2:T(8,128)(2,1)} dynamic-update-slice(bf16[16,64,1,2,4096]{4,0,1,3,2:T(8,128)(2,1)} %dynamic_update_slice.47, bf16[1,64,1,2,4096]{4,0,1,3,2:T(2,128)(2,1)S(1)} %copy.43, s32[]{:T(128)S(6)} %select_n.236, s32[]{:T(128)} %constant.205.clone.1, s32[]{:T(128)} %constant.205.clone.1, s32[]{:T(128)} %constant.205.clone.1, s32[]{:T(128)} %constant.205.clone.1) | dynamic-update-slice | bytes 2097156 | tf_op jit(solution)/shard_map/dynamic_update_slice | solution.py:28
  571.6 37.5 %dynamic_update_slice.49 = bf16[16,64,1,2,4096]{4,0,1,3,2:T(8,128)(2,1)} dynamic-update-slice(bf16[16,64,1,2,4096]{4,0,1,3,2:T(8,128)(2,1)} %dynamic_update_slice.48, bf16[1,64,1,2,4096]{4,0,1,3,2:T(2,128)(2,1)S(1)} %copy.44, s32[]{:T(128)S(6)} %select_n.240, s32[]{:T(128)} %constant.205.clone.1, s32[]{:T(128)} %constant.205.clone.1, s32[]{:T(128)} %constant.205.clone.1, s32[]{:T(128)} %constant.205.clone.1) | dynamic-update-slice | bytes 2097156 | tf_op jit(solution)/shard_map/dynamic_update_slice | solution.py:28
  612.7 37.5 %dynamic_update_slice.50 = bf16[16,64,1,2,4096]{4,0,1,3,2:T(8,128)(2,1)} dynamic-update-slice(bf16[16,64,1,2,4096]{4,0,1,3,2:T(8,128)(2,1)} %dynamic_update_slice.49, bf16[1,64,1,2,4096]{4,0,1,3,2:T(2,128)(2,1)S(1)} %copy.45, s32[]{:T(128)S(6)} %select_n.244, s32[]{:T(128)} %constant.205.clone.1, s32[]{:T(128)} %constant.205.clone.1, s32[]{:T(128)} %constant.205.clone.1, s32[]{:T(128)} %constant.205.clone.1) | dynamic-update-slice | bytes 2097156 | tf_op jit(solution)/shard_map/dynamic_update_slice | solution.py:28
  653.8 37.9 %dynamic_update_slice.51 = bf16[16,64,1,2,4096]{4,0,1,3,2:T(8,128)(2,1)} dynamic-update-slice(bf16[16,64,1,2,4096]{4,0,1,3,2:T(8,128)(2,1)} %dynamic_update_slice.50, bf16[1,64,1,2,4096]{4,0,1,3,2:T(2,128)(2,1)S(1)} %copy.46, s32[]{:T(128)S(6)} %select_n.248, s32[]{:T(128)} %constant.205.clone.1, s32[]{:T(128)} %constant.205.clone.1, s32[]{:T(128)} %constant.205.clone.1, s32[]{:T(128)} %constant.205.clone.1) | dynamic-update-slice | bytes 2097156 | tf_op jit(solution)/shard_map/dynamic_update_slice | solution.py:28
  695.3 37.5 %dynamic_update_slice.52 = bf16[16,64,1,2,4096]{4,0,1,3,2:T(8,128)(2,1)} dynamic-update-slice(bf16[16,64,1,2,4096]{4,0,1,3,2:T(8,128)(2,1)} %dynamic_update_slice.51, bf16[1,64,1,2,4096]{4,0,1,3,2:T(2,128)(2,1)S(1)} %copy.47, s32[]{:T(128)S(6)} %select_n.252, s32[]{:T(128)} %constant.205.clone.1, s32[]{:T(128)} %constant.205.clone.1, s32[]{:T(128)} %constant.205.clone.1, s32[]{:T(128)} %constant.205.clone.1) | dynamic-update-slice | bytes 2097156 | tf_op jit(solution)/shard_map/dynamic_update_slice | solution.py:28
  736.5 37.5 %dynamic_update_slice.53 = bf16[16,64,1,2,4096]{4,0,1,3,2:T(8,128)(2,1)} dynamic-update-slice(bf16[16,64,1,2,4096]{4,0,1,3,2:T(8,128)(2,1)} %dynamic_update_slice.52, bf16[1,64,1,2,4096]{4,0,1,3,2:T(2,128)(2,1)S(1)} %copy.48, s32[]{:T(128)S(6)} %select_n.256, s32[]{:T(128)} %constant.205.clone.1, s32[]{:T(128)} %constant.205.clone.1, s32[]{:T(128)} %constant.205.clone.1, s32[]{:T(128)} %constant.205.clone.1) | dynamic-update-slice | bytes 2097156 | tf_op jit(solution)/shard_map/dynamic_update_slice | solution.py:28
  777.6 37.5 %dynamic_update_slice.54 = bf16[16,64,1,2,4096]{4,0,1,3,2:T(8,128)(2,1)} dynamic-update-slice(bf16[16,64,1,2,4096]{4,0,1,3,2:T(8,128)(2,1)} %dynamic_update_slice.53, bf16[1,64,1,2,4096]{4,0,1,3,2:T(2,128)(2,1)S(1)} %copy.49, s32[]{:T(128)S(6)} %select_n.260, s32[]{:T(128)} %constant.205.clone.1, s32[]{:T(128)} %constant.205.clone.1, s32[]{:T(128)} %constant.205.clone.1, s32[]{:T(128)} %constant.205.clone.1) | dynamic-update-slice | bytes 2097156 | tf_op jit(solution)/shard_map/dynamic_update_slice | solution.py:28
  818.7 37.5 %dynamic_update_slice.55 = bf16[16,64,1,2,4096]{4,0,1,3,2:T(8,128)(2,1)} dynamic-update-slice(bf16[16,64,1,2,4096]{4,0,1,3,2:T(8,128)(2,1)} %dynamic_update_slice.54, bf16[1,64,1,2,4096]{4,0,1,3,2:T(2,128)(2,1)S(1)} %copy.50, s32[]{:T(128)S(6)} %select_n.264, s32[]{:T(128)} %constant.205.clone.1, s32[]{:T(128)} %constant.205.clone.1, s32[]{:T(128)} %constant.205.clone.1, s32[]{:T(128)} %constant.205.clone.1) | dynamic-update-slice | bytes 2097156 | tf_op jit(solution)/shard_map/dynamic_update_slice | solution.py:28
  859.8 37.5 %dynamic_update_slice.56 = bf16[16,64,1,2,4096]{4,0,1,3,2:T(8,128)(2,1)} dynamic-update-slice(bf16[16,64,1,2,4096]{4,0,1,3,2:T(8,128)(2,1)} %dynamic_update_slice.55, bf16[1,64,1,2,4096]{4,0,1,3,2:T(2,128)(2,1)S(1)} %copy.51, s32[]{:T(128)S(6)} %select_n.268, s32[]{:T(128)} %constant.205.clone.1, s32[]{:T(128)} %constant.205.clone.1, s32[]{:T(128)} %constant.205.clone.1, s32[]{:T(128)} %constant.205.clone.1) | dynamic-update-slice | bytes 2097156 | tf_op jit(solution)/shard_map/dynamic_update_slice | solution.py:28
  900.9 37.6 %dynamic_update_slice.57 = bf16[16,64,1,2,4096]{4,0,1,3,2:T(8,128)(2,1)} dynamic-update-slice(bf16[16,64,1,2,4096]{4,0,1,3,2:T(8,128)(2,1)} %dynamic_update_slice.56, bf16[1,64,1,2,4096]{4,0,1,3,2:T(2,128)(2,1)S(1)} %copy.52, s32[]{:T(128)S(6)} %select_n.272, s32[]{:T(128)} %constant.205.clone.1, s32[]{:T(128)} %constant.205.clone.1, s32[]{:T(128)} %constant.205.clone.1, s32[]{:T(128)} %constant.205.clone.1) | dynamic-update-slice | bytes 2097156 | tf_op jit(solution)/shard_map/dynamic_update_slice | solution.py:28
  942.1 37.5 %dynamic_update_slice.58 = bf16[16,64,1,2,4096]{4,0,1,3,2:T(8,128)(2,1)} dynamic-update-slice(bf16[16,64,1,2,4096]{4,0,1,3,2:T(8,128)(2,1)} %dynamic_update_slice.57, bf16[1,64,1,2,4096]{4,0,1,3,2:T(2,128)(2,1)S(1)} %copy.53, s32[]{:T(128)S(6)} %select_n.276, s32[]{:T(128)} %constant.205.clone.1, s32[]{:T(128)} %constant.205.clone.1, s32[]{:T(128)} %constant.205.clone.1, s32[]{:T(128)} %constant.205.clone.1) | dynamic-update-slice | bytes 2097156 | tf_op jit(solution)/shard_map/dynamic_update_slice | solution.py:28
  983.2 37.5 %dynamic_update_slice.59 = bf16[16,64,1,2,4096]{4,0,1,3,2:T(8,128)(2,1)} dynamic-update-slice(bf16[16,64,1,2,4096]{4,0,1,3,2:T(8,128)(2,1)} %dynamic_update_slice.58, bf16[1,64,1,2,4096]{4,0,1,3,2:T(2,128)(2,1)S(1)} %copy.54, s32[]{:T(128)S(6)} %select_n.280, s32[]{:T(128)} %constant.205.clone.1, s32[]{:T(128)} %constant.205.clone.1, s32[]{:T(128)} %constant.205.clone.1, s32[]{:T(128)} %constant.205.clone.1) | dynamic-update-slice | bytes 2097156 | tf_op jit(solution)/shard_map/dynamic_update_slice | solution.py:28
  1020.7 14.7 copy.55
  1098.1 13.7 fusion.19
  1132.0 13.5 fusion.22
  1157.2 170.3 %collective-permute-done.15 = bf16[1024,32,128]{2,0,1:T(8,128)(2,1)} collective-permute-done((bf16[1024,32,128]{2,0,1:T(8,128)(2,1)}, bf16[1024,32,128]{2,0,1:T(8,128)(2,1)}, u32[]{:S(2)}, u32[]{:S(2)}) %collective-permute-start.15) | collective-permute-done | bytes 8388640 | tf_op jit(solution)/shard_map/ppermute | solution.py:39
  1336.1 13.6 fusion.25
  1370.3 13.6 fusion.28
  1406.8 13.6 fusion.31
  1440.7 13.7 fusion.34
  1479.9 187.5 %all_to_all.19 = bf16[16,64,4096]{2,1,0:T(8,128)(2,1)} all-to-all(bf16[16,64,4096]{2,1,0:T(8,128)(2,1)} %all_to_all.14), channel_id=1, replica_groups=mesh['groups'=2,'slab'=16] {'slab'}, dimensions={0} | all-to-all | bytes 16777216 | tf_op jit(solution)/shard_map/all_to_all | solution.py:84
  (117 shorter events, 340.7 us)
Async XLA Ops:
  47.5 58.0 %collective-permute-start = (bf16[1,64,1,2,4096]{4,1,3,2,0:T(8,128)(2,1)}, bf16[1,64,1,2,4096]{4,1,3,2,0:T(8,128)(2,1)S(1)}, u32[]{:S(2)}, u32[]{:S(2)}) collective-permute-start(bf16[1,64,1,2,4096]{4,1,3,2,0:T(8,128)(2,1)} %bitcast.172), channel_id=1, source_target_pairs={{0,1},{1,2},{2,3},{3,4},{4,5},{5,6},{6,7},{7,8},{8,9},{9,10},{10,1... | collective-permute-start | bytes 3145736 | tf_op jit(solution)/shard_map/ppermute | solution.py:27
  52.2 55.0 %collective-permute-start.1 = (bf16[1,64,1,2,4096]{4,1,3,2,0:T(8,128)(2,1)}, bf16[1,64,1,2,4096]{4,1,3,2,0:T(8,128)(2,1)}, u32[]{:S(2)}, u32[]{:S(2)}) collective-permute-start(bf16[1,64,1,2,4096]{4,1,3,2,0:T(8,128)(2,1)} %bitcast.171), channel_id=1, source_target_pairs={{0,2},{1,3},{2,4},{3,5},{4,6},{5,7},{6,8},{7,9},{8,10},{9,11},{10,... | collective-permute-start | bytes 3145736 | tf_op jit(solution)/shard_map/ppermute | solution.py:27
  54.8 54.1 %collective-permute-start.2 = (bf16[1,64,1,2,4096]{4,1,3,2,0:T(8,128)(2,1)}, bf16[1,64,1,2,4096]{4,1,3,2,0:T(8,128)(2,1)}, u32[]{:S(2)}, u32[]{:S(2)}) collective-permute-start(bf16[1,64,1,2,4096]{4,1,3,2,0:T(8,128)(2,1)} %bitcast.170), channel_id=1, source_target_pairs={{0,3},{1,4},{2,5},{3,6},{4,7},{5,8},{6,9},{7,10},{8,11},{9,12},{10... | collective-permute-start | bytes 3145736 | tf_op jit(solution)/shard_map/ppermute | solution.py:27
  57.3 51.7 %collective-permute-start.3 = (bf16[1,64,1,2,4096]{4,1,3,2,0:T(8,128)(2,1)}, bf16[1,64,1,2,4096]{4,1,3,2,0:T(8,128)(2,1)}, u32[]{:S(2)}, u32[]{:S(2)}) collective-permute-start(bf16[1,64,1,2,4096]{4,1,3,2,0:T(8,128)(2,1)} %bitcast.169), channel_id=1, source_target_pairs={{0,4},{1,5},{2,6},{3,7},{4,8},{5,9},{6,10},{7,11},{8,12},{9,13},{1... | collective-permute-start | bytes 3145736 | tf_op jit(solution)/shard_map/ppermute | solution.py:27
  61.8 63.9 %collective-permute-start.4 = (bf16[1,64,1,2,4096]{4,1,3,2,0:T(8,128)(2,1)}, bf16[1,64,1,2,4096]{4,1,3,2,0:T(8,128)(2,1)}, u32[]{:S(2)}, u32[]{:S(2)}) collective-permute-start(bf16[1,64,1,2,4096]{4,1,3,2,0:T(8,128)(2,1)} %bitcast.168), channel_id=1, source_target_pairs={{0,5},{1,6},{2,7},{3,8},{4,9},{5,10},{6,11},{7,12},{8,13},{9,14},{... | collective-permute-start | bytes 3145736 | tf_op jit(solution)/shard_map/ppermute | solution.py:27
  89.8 11.4 copy-start.2
  89.8 13.5 copy-start.1
  105.5 207.2 %collective-permute-start.5 = (bf16[1,64,1,2,4096]{4,1,3,2,0:T(8,128)(2,1)}, bf16[1,64,1,2,4096]{4,1,3,2,0:T(8,128)(2,1)}, u32[]{:S(2)}, u32[]{:S(2)}) collective-permute-start(bf16[1,64,1,2,4096]{4,1,3,2,0:T(8,128)(2,1)} %bitcast.191), channel_id=1, source_target_pairs={{0,6},{1,7},{2,8},{3,9},{4,10},{5,11},{6,12},{7,13},{8,14},{9,15},... | collective-permute-start | bytes 3145736 | tf_op jit(solution)/shard_map/ppermute | solution.py:27
  107.3 221.7 %collective-permute-start.6 = (bf16[1,64,1,2,4096]{4,1,3,2,0:T(8,128)(2,1)}, bf16[1,64,1,2,4096]{4,1,3,2,0:T(8,128)(2,1)}, u32[]{:S(2)}, u32[]{:S(2)}) collective-permute-start(bf16[1,64,1,2,4096]{4,1,3,2,0:T(8,128)(2,1)} %bitcast.190), channel_id=1, source_target_pairs={{0,7},{1,8},{2,9},{3,10},{4,11},{5,12},{6,13},{7,14},{8,15},{9,0},... | collective-permute-start | bytes 3145736 | tf_op jit(solution)/shard_map/ppermute | solution.py:27
  109.0 242.0 %collective-permute-start.7 = (bf16[1,64,1,2,4096]{4,1,3,2,0:T(8,128)(2,1)}, bf16[1,64,1,2,4096]{4,1,3,2,0:T(8,128)(2,1)}, u32[]{:S(2)}, u32[]{:S(2)}) collective-permute-start(bf16[1,64,1,2,4096]{4,1,3,2,0:T(8,128)(2,1)} %bitcast.189), channel_id=1, source_target_pairs={{0,8},{1,9},{2,10},{3,11},{4,12},{5,13},{6,14},{7,15},{8,0},{9,1},... | collective-permute-start | bytes 3145736 | tf_op jit(solution)/shard_map/ppermute | solution.py:27
  109.0 276.0 %collective-permute-start.8 = (bf16[1,64,1,2,4096]{4,1,3,2,0:T(8,128)(2,1)}, bf16[1,64,1,2,4096]{4,1,3,2,0:T(8,128)(2,1)}, u32[]{:S(2)}, u32[]{:S(2)}) collective-permute-start(bf16[1,64,1,2,4096]{4,1,3,2,0:T(8,128)(2,1)} %bitcast.188), channel_id=1, source_target_pairs={{0,9},{1,10},{2,11},{3,12},{4,13},{5,14},{6,15},{7,0},{8,1},{9,2},... | collective-permute-start | bytes 3145736 | tf_op jit(solution)/shard_map/ppermute | solution.py:27
  125.6 180.2 %slice-start.2 = ((s8[8388608]{0:T(1024)(128)(4,1)}), s8[4194304]{0:T(1024)(128)(4,1)S(1)}, s32[]{:S(2)}) async-start(s8[8388608]{0:T(1024)(128)(4,1)} %bitcast.180), calls=%async_computation.3 | async-start | bytes 8388608
  125.6 180.2 %slice-start.3 = ((s8[8388608]{0:T(1024)(128)(4,1)}), s8[4194304]{0:T(1024)(128)(4,1)S(1)}, s32[]{:S(2)}) async-start(s8[8388608]{0:T(1024)(128)(4,1)} %bitcast.180), calls=%async_computation.4 | async-start | bytes 8388608
  125.6 277.6 %collective-permute-start.9 = (bf16[1,64,1,2,4096]{4,1,3,2,0:T(8,128)(2,1)}, bf16[1,64,1,2,4096]{4,1,3,2,0:T(8,128)(2,1)}, u32[]{:S(2)}, u32[]{:S(2)}) collective-permute-start(bf16[1,64,1,2,4096]{4,1,3,2,0:T(8,128)(2,1)} %bitcast.187), channel_id=1, source_target_pairs={{0,10},{1,11},{2,12},{3,13},{4,14},{5,15},{6,0},{7,1},{8,2},{9,3},... | collective-permute-start | bytes 3145736 | tf_op jit(solution)/shard_map/ppermute | solution.py:27
  295.2 6.4 copy-start
  295.2 10.7 slice-start
  299.5 6.4 slice-start.1
  305.9 97.4 %copy-start.6 = (s32[6,32]{1,0:T(8,128)S(1)}, s32[6,32]{1,0:T(8,128)}, u32[]{:S(2)}) copy-start(s32[6,32]{1,0:T(8,128)} %param.9) | copy-start | bytes 2308
  305.9 98.0 %copy-start.3 = (f32[6,4096]{1,0:T(8,128)S(1)}, f32[6,4096]{1,0:T(8,128)}, u32[]{:S(2)}) copy-start(f32[6,4096]{1,0:T(8,128)} %param.8) | copy-start | bytes 294916
  312.6 502.4 %collective-permute-start.10 = (bf16[1,64,1,2,4096]{4,1,3,2,0:T(8,128)(2,1)}, bf16[1,64,1,2,4096]{4,1,3,2,0:T(8,128)(2,1)}, u32[]{:S(2)}, u32[]{:S(2)}) collective-permute-start(bf16[1,64,1,2,4096]{4,1,3,2,0:T(8,128)(2,1)} %bitcast.162), channel_id=1, source_target_pairs={{0,11},{1,12},{2,13},{3,14},{4,15},{5,0},{6,1},{7,2},{8,3},{9,4},{... | collective-permute-start | bytes 3145736 | tf_op jit(solution)/shard_map/ppermute | solution.py:27
  329.0 527.2 %collective-permute-start.11 = (bf16[1,64,1,2,4096]{4,1,3,2,0:T(8,128)(2,1)}, bf16[1,64,1,2,4096]{4,1,3,2,0:T(8,128)(2,1)}, u32[]{:S(2)}, u32[]{:S(2)}) collective-permute-start(bf16[1,64,1,2,4096]{4,1,3,2,0:T(8,128)(2,1)} %bitcast.161), channel_id=1, source_target_pairs={{0,12},{1,13},{2,14},{3,15},{4,0},{5,1},{6,2},{7,3},{8,4},{9,5},{1... | collective-permute-start | bytes 3145736 | tf_op jit(solution)/shard_map/ppermute | solution.py:27
  350.9 546.3 %collective-permute-start.12 = (bf16[1,64,1,2,4096]{4,1,3,2,0:T(8,128)(2,1)}, bf16[1,64,1,2,4096]{4,1,3,2,0:T(8,128)(2,1)}, u32[]{:S(2)}, u32[]{:S(2)}) collective-permute-start(bf16[1,64,1,2,4096]{4,1,3,2,0:T(8,128)(2,1)} %bitcast.160), channel_id=1, source_target_pairs={{0,13},{1,14},{2,15},{3,0},{4,1},{5,2},{6,3},{7,4},{8,5},{9,6},{10... | collective-permute-start | bytes 3145736 | tf_op jit(solution)/shard_map/ppermute | solution.py:27
  384.9 553.6 %collective-permute-start.13 = (bf16[1,64,1,2,4096]{4,1,3,2,0:T(8,128)(2,1)}, bf16[1,64,1,2,4096]{4,1,3,2,0:T(8,128)(2,1)}, u32[]{:S(2)}, u32[]{:S(2)}) collective-permute-start(bf16[1,64,1,2,4096]{4,1,3,2,0:T(8,128)(2,1)} %bitcast.159), channel_id=1, source_target_pairs={{0,14},{1,15},{2,0},{3,1},{4,2},{5,3},{6,4},{7,5},{8,6},{9,7},{10,... | collective-permute-start | bytes 3145736 | tf_op jit(solution)/shard_map/ppermute | solution.py:27
  403.3 576.4 %collective-permute-start.14 = (bf16[1,64,1,2,4096]{4,1,3,2,0:T(8,128)(2,1)}, bf16[1,64,1,2,4096]{4,1,3,2,0:T(8,128)(2,1)}, u32[]{:S(2)}, u32[]{:S(2)}) collective-permute-start(bf16[1,64,1,2,4096]{4,1,3,2,0:T(8,128)(2,1)} %bitcast.158), channel_id=1, source_target_pairs={{0,15},{1,0},{2,1},{3,2},{4,3},{5,4},{6,5},{7,6},{8,7},{9,8},{10,9... | collective-permute-start | bytes 3145736 | tf_op jit(solution)/shard_map/ppermute | solution.py:27
  1145.5 182.0 %collective-permute-start.15 = (bf16[1024,32,128]{2,0,1:T(8,128)(2,1)}, bf16[1024,32,128]{2,0,1:T(8,128)(2,1)}, u32[]{:S(2)}, u32[]{:S(2)}) collective-permute-start(bf16[1024,32,128]{2,0,1:T(8,128)(2,1)} %fusion.22), channel_id=1, source_target_pairs={{0,2},{2,0},{1,3},{3,1},{4,6},{6,4},{5,7},{7,5},{8,10},{10,8},{9,1... | collective-permute-start | bytes 25165832 | tf_op jit(solution)/shard_map/ppermute | solution.py:39
  1370.3 14.8 copy-start.9
  1370.3 14.8 copy-start.10
  1383.9 14.4 collective-permute-start.16
  1398.2 8.6 copy-start.5
  1398.2 8.6 copy-start.8
  1432.1 8.6 copy-start.4
  1432.1 8.6 copy-start.7
